TPU v7x, 32 devices: a whole 2x2x4 slice. The times are simulated.
32 devices in a mesh: row: 8 (over z, y), col: 4 (over x, core).
Axes of the slice: x: 2, y: 2, z: 4, core: 2. Of those that a mesh axis runs over, the one named last changes fastest.
Arguments:
- tokens_in: bfloat16 [192, 8192], P('row', 'col'), may hold values from -6 to 6
- gate_weight: bfloat16 [8192, 28672], P('col', 'row'), may hold values from -0.0625 to 0.0625
- up_weight: bfloat16 [8192, 28672], P('col', 'row'), may hold values from -0.0625 to 0.0625
- down_weight: bfloat16 [28672, 8192], P('row', 'col'), may hold values from -0.03125 to 0.03125
- out_grad: bfloat16 [192, 8192], P('row', 'col'), may hold values from -0.29882812 to 0.29882812
Outputs:
- output: bfloat16 [192, 8192], P('row', 'col')
- in_grad: bfloat16 [192, 8192], P('row', 'col')
- gate_grad: bfloat16 [8192, 28672], P('col', 'row')
- up_grad: bfloat16 [8192, 28672], P('col', 'row')
- down_grad: bfloat16 [28672, 8192], P('row', 'col')
All inputs are finite; a program needn't handle non-finite values.
Results may differ from a plain program's by a relative error of at most 0.0051.
Values may be sent and summed in bfloat16 or wider, within the bound.
A program may use at most 192 MiB of HBM per device.

v0:
```python
import jax
import jax.numpy as jnp
from jax import lax
from jax.sharding import PartitionSpec as P


def contract_last(left, right):
    return lax.dot_general(
        left, right, (((1,), (1,)), ((), ())), preferred_element_type=jnp.float32
    )


def contract_first(left, right):
    return lax.dot_general(
        left, right, (((0,), (0,)), ((), ())), preferred_element_type=jnp.float32
    )


def forward_gate(gate_pre, up_pre):
    sigma_gate = jax.nn.sigmoid(gate_pre)
    activated = gate_pre * sigma_gate
    hidden = (activated * up_pre).astype(jnp.bfloat16)
    return (hidden, sigma_gate, activated)


def backward_gate(d_hidden, gate_pre, up_pre, sigma_gate, activated):
    d_gate = (d_hidden * up_pre * sigma_gate * (1.0 + gate_pre * (1.0 - sigma_gate))).astype(
        jnp.bfloat16
    )
    d_up = (d_hidden * activated).astype(jnp.bfloat16)
    return (d_gate, d_up)


def shards(tokens_in, gate_weight, up_weight, down_weight, out_grad):
    inputs_all = lax.all_gather(tokens_in, "row", axis=0, tiled=True)
    gate_part = jnp.dot(inputs_all, gate_weight, preferred_element_type=jnp.float32)
    up_part = jnp.dot(inputs_all, up_weight, preferred_element_type=jnp.float32)
    gate_pre, up_pre = (
        lax.psum_scatter(gate_part, "col", scatter_dimension=0, tiled=True),
        lax.psum_scatter(up_part, "col", scatter_dimension=0, tiled=True),
    )
    hidden_share, sigma_gate, activated = forward_gate(gate_pre, up_pre)
    hidden_all = lax.all_gather(hidden_share, "col", axis=0, tiled=True)
    output = lax.psum_scatter(
        jnp.dot(hidden_all, down_weight, preferred_element_type=jnp.float32),
        "row",
        scatter_dimension=0,
        tiled=True,
    ).astype(jnp.bfloat16)
    grad_all = lax.all_gather(out_grad, "row", axis=0, tiled=True)
    dhid_part = contract_last(grad_all, down_weight)
    d_hidden = lax.psum_scatter(dhid_part, "col", scatter_dimension=0, tiled=True)
    d_gate, d_up = backward_gate(d_hidden, gate_pre, up_pre, sigma_gate, activated)
    d_gate_all, d_up_all = (
        lax.all_gather(d_gate, "col", axis=0, tiled=True),
        lax.all_gather(d_up, "col", axis=0, tiled=True),
    )
    in_grad = lax.psum_scatter(
        contract_last(d_gate_all, gate_weight) + contract_last(d_up_all, up_weight),
        "row",
        scatter_dimension=0,
        tiled=True,
    ).astype(jnp.bfloat16)
    gate_grad = contract_first(inputs_all, d_gate_all).astype(jnp.bfloat16)
    up_grad = contract_first(inputs_all, d_up_all).astype(jnp.bfloat16)
    down_grad = contract_first(hidden_all, grad_all).astype(jnp.bfloat16)
    return (output, in_grad, gate_grad, up_grad, down_grad)


def solution(mesh):
    in_specs = (P("row", "col"), P("col", "row"), P("col", "row"), P("row", "col"), P("row", "col"))
    out_specs = (
        P("row", "col"),
        P("row", "col"),
        P("col", "row"),
        P("col", "row"),
        P("row", "col"),
    )
    return jax.shard_map(shards, mesh=mesh, in_specs=in_specs, out_specs=out_specs, check_vma=False)
```

profile of v0, /device:TPU:0, one launch (start us, length us, event | category | flops | bytes accessed | tf_op | source)
XLA Modules:
  0.0 378.7 jit_solution(6762438291876996533)
XLA Ops:
  7.2 0.0 reduce-scatter.12.cloned.1.call-start
  7.2 34.1 %all_gather.17 = bf16[192,2048]{1,0:T(8,128)(2,1)S(1)} all-gather(bf16[24,2048]{1,0:T(8,128)(2,1)} %param.9), channel_id=1, replica_groups=mesh['row'=8,'col'=4] {'row'}, dimensions={0}, use_global_device_ids=true | all-gather | bytes 884736 | tf_op jit(solution)/shard_map/all_gather | solution.py:50
  41.3 11.7 %fusion.6 = f32[192,3584]{1,0:T(8,128)} fusion(bf16[192,2048]{1,0:T(8,128)(2,1)S(1)} %all_gather.17, bf16[3584,2048]{1,0:T(8,128)(2,1)} %param.8), kind=kOutput, calls=%fused_computation.14 | convolution fusion | flops 2818572288 | bytes 18219008 | tf_op jit(solution)/shard_map/dot_general | solution.py:8
  53.0 0.0 copy-start.3
  53.0 0.0 reduce-scatter.12.cloned.1.call-update
  53.0 0.0 reduce-scatter.6.cloned.1.call-start
  53.1 0.8 copy-done.3
  53.9 32.1 %all_gather.15 = bf16[192,2048]{1,0:T(8,128)(2,1)S(1)} all-gather(bf16[24,2048]{1,0:T(8,128)(2,1)S(1)} %copy-done.3), channel_id=1, replica_groups=mesh['row'=8,'col'=4] {'row'}, dimensions={0}, use_global_device_ids=true | all-gather | bytes 884736 | tf_op jit(solution)/shard_map/all_gather | solution.py:35
  86.0 9.8 %fusion.3 = f32[192,3584]{1,0:T(8,128)} fusion(bf16[192,2048]{1,0:T(8,128)(2,1)S(1)} %all_gather.15, bf16[2048,3584]{1,0:T(8,128)(2,1)} %param.6), kind=kOutput, calls=%fused_computation.11 | convolution fusion | flops 2818572288 | bytes 18219008 | tf_op jit(solution)/shard_map/dot_general | solution.py:36
  95.8 0.0 reduce-scatter.6.cloned.1.call-update
  95.8 0.0 reduce-scatter.8.cloned.1.call-start
  95.8 9.7 %fusion.4 = f32[192,3584]{1,0:T(8,128)} fusion(bf16[192,2048]{1,0:T(8,128)(2,1)S(1)} %all_gather.15, bf16[2048,3584]{1,0:T(8,128)(2,1)} %param.7), kind=kOutput, calls=%fused_computation.12 | convolution fusion | flops 2818572288 | bytes 18219008 | tf_op jit(solution)/shard_map/dot_general | solution.py:37
  105.5 0.0 reduce-scatter.8.cloned.1.call-update
  105.6 0.0 all-gather.4.cloned.1.call-start
  105.6 0.0 reduce-scatter.12.cloned.1.call-done
  105.6 26.5 %reduce-scatter.6.cloned.1.call-done = f32[48,3584]{1,0:T(8,128)} async-done(((f32[192,3584]{1,0:T(8,128)}), f32[48,3584]{1,0:T(8,128)}) %reduce-scatter.6.cloned.1.call-update) | async-done | bytes 688144 | tf_op jit(solution)/shard_map/reduce_scatter | solution.py:39
  132.1 38.5 %reduce-scatter.8.cloned.1.call-done = f32[48,3584]{1,0:T(8,128)} async-done(((f32[192,3584]{1,0:T(8,128)}), f32[48,3584]{1,0:T(8,128)}) %reduce-scatter.8.cloned.1.call-update) | async-done | bytes 688144 | tf_op jit(solution)/shard_map/reduce_scatter | solution.py:40
  170.7 2.8 multiply_convert_fusion
  173.4 0.0 all-gather.4.cloned.1.call-update
  173.5 0.0 all-gather.6.cloned.1.call-start
  173.5 0.5 all-gather.6.cloned.1.call-update
  174.1 0.0 all-gather.8.cloned.1.call-start
  174.1 0.5 all-gather.8.cloned.1.call-update
  174.6 0.0 reduce-scatter.10.cloned.1.call-start
  174.7 17.5 %all-gather.4.cloned.1.call-done = bf16[192,3584]{1,0:T(8,128)(2,1)} async-done(((bf16[48,3584]{1,0:T(8,128)(2,1)}), bf16[192,3584]{1,0:T(8,128)(2,1)}) %all-gather.4.cloned.1.call-update) | async-done | bytes 1376272 | tf_op jit(solution)/shard_map/all_gather | solution.py:43
  192.2 9.8 %fusion.5 = f32[192,2048]{1,0:T(8,128)} fusion(bf16[192,3584]{1,0:T(8,128)(2,1)} %all-gather.4.cloned.1.call-done, bf16[3584,2048]{1,0:T(8,128)(2,1)} %param.8), kind=kOutput, calls=%fused_computation.13 | convolution fusion | flops 2818572288 | bytes 17629184 | tf_op jit(solution)/shard_map/dot_general | solution.py:45
  201.9 0.0 reduce-scatter.10.cloned.1.call-update
  202.0 0.2 reduce-scatter.14.cloned.1.call-start
  202.2 10.5 %all-gather.6.cloned.1.call-done = bf16[192,3584]{1,0:T(8,128)(2,1)} async-done(((bf16[48,3584]{1,0:T(8,128)(2,1)}), bf16[192,3584]{1,0:T(8,128)(2,1)}) %all-gather.6.cloned.1.call-update) | async-done | bytes 1376272 | tf_op jit(solution)/shard_map/all_gather | solution.py:55
  212.7 8.5 %fusion.7 = f32[192,2048]{1,0:T(8,128)S(1)} fusion(bf16[192,3584]{1,0:T(8,128)(2,1)} %all-gather.6.cloned.1.call-done, bf16[2048,3584]{1,0:T(8,128)(2,1)} %param.6), kind=kOutput, calls=%fused_computation.15 | convolution fusion | flops 2818572288 | bytes 17629184 | tf_op jit(solution)/shard_map/dot_general | solution.py:8
  221.2 12.1 %all-gather.8.cloned.1.call-done = bf16[192,3584]{1,0:T(8,128)(2,1)} async-done(((bf16[48,3584]{1,0:T(8,128)(2,1)}), bf16[192,3584]{1,0:T(8,128)(2,1)}) %all-gather.8.cloned.1.call-update) | async-done | bytes 1376272 | tf_op jit(solution)/shard_map/all_gather | solution.py:56
  233.3 11.6 %convolution_add_fusion = f32[192,2048]{1,0:T(8,128)} fusion(f32[192,2048]{1,0:T(8,128)S(1)} %fusion.7, bf16[192,3584]{1,0:T(8,128)(2,1)} %all-gather.8.cloned.1.call-done, bf16[2048,3584]{1,0:T(8,128)(2,1)} %param.7), kind=kOutput, calls=%fused_computation.5 | convolution fusion | flops 2818965504 | bytes 19202048 | tf_op jit(solution)/shard_map/dot_general | solution.py:8
  244.9 0.0 copy-start.1
  244.9 0.0 reduce-scatter.14.cloned.1.call-update
  244.9 1.3 copy-done.1
  246.2 7.6 %fusion = bf16[2048,3584]{0,1:T(8,128)(2,1)} fusion(bf16[192,3584]{1,0:T(8,128)(2,1)S(1)} %copy-done.1, bf16[192,2048]{1,0:T(8,128)(2,1)S(1)} %all_gather.15), kind=kOutput, calls=%fused_computation.3 | convolution fusion | flops 2825912320 | bytes 16842752 | tf_op jit(solution)/shard_map/dot_general | solution.py:14
  253.8 0.0 copy-start.2
  253.8 18.8 %copy.10 = bf16[2048,3584]{1,0:T(8,128)(2,1)} copy(bf16[2048,3584]{0,1:T(8,128)(2,1)} %fusion) | data formatting | bytes 29360128
  272.6 0.0 copy-done.2
  272.6 7.6 %fusion.1 = bf16[2048,3584]{0,1:T(8,128)(2,1)} fusion(bf16[192,3584]{1,0:T(8,128)(2,1)S(1)} %copy-done.2, bf16[192,2048]{1,0:T(8,128)(2,1)S(1)} %all_gather.15), kind=kOutput, calls=%fused_computation.4 | convolution fusion | flops 2825912320 | bytes 16842752 | tf_op jit(solution)/shard_map/dot_general | solution.py:14
  280.2 0.0 copy-start
  280.2 18.8 %copy.11 = bf16[2048,3584]{1,0:T(8,128)(2,1)} copy(bf16[2048,3584]{0,1:T(8,128)(2,1)} %fusion.1) | data formatting | bytes 29360128
  299.0 0.0 copy-done
  299.0 7.6 %convolution_convert_fusion = bf16[3584,2048]{1,0:T(8,128)(2,1)} fusion(bf16[192,3584]{1,0:T(8,128)(2,1)S(1)} %copy-done, bf16[192,2048]{1,0:T(8,128)(2,1)S(1)} %all_gather.17), kind=kOutput, calls=%fused_computation | convolution fusion | flops 2825912320 | bytes 16842752 | tf_op jit(solution)/shard_map/dot_general | solution.py:14
  306.6 0.0 reduce-scatter.10.cloned.1.call-done
  306.6 1.6 convert_element_type.31
  308.2 62.1 %reduce-scatter.14.cloned.1.call-done = f32[24,2048]{1,0:T(8,128)} async-done(((f32[192,2048]{1,0:T(8,128)}), f32[24,2048]{1,0:T(8,128)}) %reduce-scatter.14.cloned.1.call-update) | async-done | bytes 196624 | tf_op jit(solution)/shard_map/reduce_scatter | solution.py:58
  370.3 1.6 convert_element_type.34
Async XLA Ops:
  7.2 98.5 %reduce-scatter.12.cloned.1.call-start = ((), (), s32[]{:S(2)}) async-start(), calls=%async_computation.9 | async-start | bytes 3440640 | tf_op jit(solution)/shard_map/reduce_scatter | solution.py:52
  53.0 0.9 copy-start.3
  53.0 79.1 %reduce-scatter.6.cloned.1.call-start = ((), (), s32[]{:S(2)}) async-start(), calls=%async_computation.5 | async-start | bytes 3440640 | tf_op jit(solution)/shard_map/reduce_scatter | solution.py:39
  95.8 74.9 %reduce-scatter.8.cloned.1.call-start = ((), (), s32[]{:S(2)}) async-start(), calls=%async_computation.6 | async-start | bytes 3440640 | tf_op jit(solution)/shard_map/reduce_scatter | solution.py:40
  105.6 86.6 %all-gather.4.cloned.1.call-start = ((), (), s32[]{:S(2)}) async-start(), calls=%async_computation.7 | async-start | bytes 1720320 | tf_op jit(solution)/shard_map/all_gather | solution.py:43
  173.5 39.2 %all-gather.6.cloned.1.call-start = ((), (), s32[]{:S(2)}) async-start(), calls=%async_computation.10 | async-start | bytes 1720320 | tf_op jit(solution)/shard_map/all_gather | solution.py:55
  174.1 59.2 %all-gather.8.cloned.1.call-start = ((), (), s32[]{:S(2)}) async-start(), calls=%async_computation.11 | async-start | bytes 1720320 | tf_op jit(solution)/shard_map/all_gather | solution.py:56
  174.6 132.0 %reduce-scatter.10.cloned.1.call-start = ((), (), s32[]{:S(2)}) async-start(), calls=%async_computation.8 | async-start | bytes 1769472 | tf_op jit(solution)/shard_map/reduce_scatter | solution.py:44
  202.0 168.3 %reduce-scatter.14.cloned.1.call-start = ((), (), s32[]{:S(2)}) async-start(), calls=%async_computation.12 | async-start | bytes 1769472 | tf_op jit(solution)/shard_map/reduce_scatter | solution.py:58
  244.9 1.3 copy-start.1
  253.8 18.8 %copy-start.2 = (bf16[192,3584]{1,0:T(8,128)(2,1)S(1)}, bf16[192,3584]{1,0:T(8,128)(2,1)}, u32[]{:S(2)}) copy-start(bf16[192,3584]{1,0:T(8,128)(2,1)} %all-gather.8.cloned.1.call-done) | copy-start | bytes 4128772
  280.2 18.8 %copy-start = (bf16[192,3584]{1,0:T(8,128)(2,1)S(1)}, bf16[192,3584]{1,0:T(8,128)(2,1)}, u32[]{:S(2)}) copy-start(bf16[192,3584]{1,0:T(8,128)(2,1)} %all-gather.4.cloned.1.call-done) | copy-start | bytes 4128772
Sparse Core Ops, SparseCore 0:
  53.1 36.2 reduce-scatter.11
  95.9 36.1 reduce-scatter.5
  135.3 35.3 reduce-scatter.7
  173.6 18.5 all-gather.3
  194.1 18.5 all-gather.5
  214.7 18.5 all-gather.7
  236.7 65.4 reduce-scatter.9
  305.6 64.6 reduce-scatter.13
where the time goes:
time: 380 us; the launch traced here: 379 us
  waiting for transfers between devices  168 us (44%)
  matrix products  83.8 us (22%)
  blocking collectives  66.2 us (17%)
  local copies, waits for them, and re-layouts  39.7 us (10%)
  between operations  14.2 us (4%)
  other arithmetic  5.93 us (2%)
    reduce_scatter x1, waiting for transfers between devices, shards(): lax.psum_scatter(contract_last(d_gate_all, gate_weight) + contract_last(d...  62.1 us
    unnamed x10, local copies, waits for them, and re-layouts  39.7 us
    reduce_scatter x1, waiting for transfers between devices, shards(): lax.psum_scatter(up_part, 'col', scatter_dimension=0, tiled=True)  38.5 us
    all_gather x1, blocking collectives, shards(): grad_all = lax.all_gather(out_grad, 'row', axis=0, tiled=True)  34.1 us
    all_gather x1, blocking collectives, shards(): inputs_all = lax.all_gather(tokens_in, 'row', axis=0, tiled=True)  32.1 us
    dot_general x3, matrix products, contract_last(): lax.dot_general(left, right, (((1,), (1,)), ((), ())), preferred_element_...  31.8 us
    reduce_scatter x1, waiting for transfers between devices, shards(): lax.psum_scatter(gate_part, 'col', scatter_dimension=0, tiled=True)  26.5 us
    dot_general x3, matrix products, contract_first(): lax.dot_general(left, right, (((0,), (0,)), ((), ())), preferred_element_...  22.8 us
  transfers between devices with their start and end apart: 8, of which 6 were waited for; matrix products, arithmetic and copies ran while one was open for 29% of the time, Pallas kernels for 0%

commit v1 on v0

--- a/solution.py
+++ b/solution.py
@@ -2,6 +2,11 @@
 import jax.numpy as jnp
 from jax import lax
 from jax.sharding import PartitionSpec as P
+
+
+def gather_by_exchange(x, axis, dim):
+    copies = jnp.concatenate([x] * lax.axis_size(axis), axis=dim)
+    return lax.all_to_all(copies, axis, dim, dim, tiled=True)
 
 
 def contract_last(left, right):
@@ -32,7 +37,7 @@
 
 
 def shards(tokens_in, gate_weight, up_weight, down_weight, out_grad):
-    inputs_all = lax.all_gather(tokens_in, "row", axis=0, tiled=True)
+    inputs_all = gather_by_exchange(tokens_in, "row", 0)
     gate_part = jnp.dot(inputs_all, gate_weight, preferred_element_type=jnp.float32)
     up_part = jnp.dot(inputs_all, up_weight, preferred_element_type=jnp.float32)
     gate_pre, up_pre = (

time: 380 us -> 375 us (0.987)
  waiting for transfers between devices: 168 us -> 212 us
  local copies, waits for them, and re-layouts: 39.7 us -> 0.9 us
  blocking collectives: 66.2 us -> 53.7 us
    unnamed x10 -> x15, local copies, waits for them, and re-layouts: 39.7 us -> 0.89 us
    reduce_scatter x1, waiting for transfers between devices: 0.01 us -> 34.2 us  [shards(): lax.psum_scatter(jnp.dot(hidden_all, down_weight, preferred_element_type=...]
    all_gather x1 -> x0, blocking collectives: 32.1 us -> none  [shards(): inputs_all = lax.all_gather(tokens_in, 'row', axis=0, tiled=True)]
    all_to_all x0 -> x1, blocking collectives: none -> 19.7 us  [gather_by_exchange(): return lax.all_to_all(copies, axis, dim, dim, tiled=True)]
    reduce_scatter x1, waiting for transfers between devices: 26.5 us -> 38.5 us  [shards(): lax.psum_scatter(gate_part, 'col', scatter_dimension=0, tiled=True)]
    reduce_scatter x1, waiting for transfers between devices: 62.1 us -> 66.4 us  [shards(): lax.psum_scatter(contract_last(d_gate_all, gate_weight) + contract_last(d...]
    reduce_scatter x1, waiting for transfers between devices: 38.5 us -> 34.6 us  [shards(): lax.psum_scatter(up_part, 'col', scatter_dimension=0, tiled=True)]
  transfers between devices with their start and end apart: 8 -> 8, of which waited for: 6 -> 7; matrix products, arithmetic and copies ran while one was open for 29% -> 21% of each run, Pallas kernels for 0% -> 0%
where the time goes in v1:
time: 375 us
  waiting for transfers between devices  212 us (57%)
  matrix products  87.5 us (23%)
  blocking collectives  53.7 us (14%)
  between operations  14.2 us (4%)
  other arithmetic  5.93 us (2%)
    reduce_scatter x1, waiting for transfers between devices, shards(): lax.psum_scatter(contract_last(d_gate_all, gate_weight) + contract_last(d...  66.4 us
    reduce_scatter x1, waiting for transfers between devices, shards(): lax.psum_scatter(gate_part, 'col', scatter_dimension=0, tiled=True)  38.5 us
    dot_general x3, matrix products, contract_last(): lax.dot_general(left, right, (((1,), (1,)), ((), ())), preferred_element_...  35.4 us
    reduce_scatter x1, waiting for transfers between devices, shards(): lax.psum_scatter(up_part, 'col', scatter_dimension=0, tiled=True)  34.6 us
    reduce_scatter x1, waiting for transfers between devices, shards(): lax.psum_scatter(jnp.dot(hidden_all, down_weight, preferred_element_type=...  34.2 us
    all_gather x1, blocking collectives, shards(): grad_all = lax.all_gather(out_grad, 'row', axis=0, tiled=True)  34.1 us
    dot_general x3, matrix products, contract_first(): lax.dot_general(left, right, (((0,), (0,)), ((), ())), preferred_element_...  22.8 us
    all_to_all x1, blocking collectives, gather_by_exchange(): return lax.all_to_all(copies, axis, dim, dim, tiled=True)  19.7 us
  transfers between devices with their start and end apart: 8, of which 7 were waited for; matrix products, arithmetic and copies ran while one was open for 21% of the time, Pallas kernels for 0%

profile of v1, /device:TPU:0, one launch (start us, length us, event | category | flops | bytes accessed | tf_op | source)
XLA Modules:
  0.0 374.6 jit_solution(9104480249063903465)
XLA Ops:
  7.2 0.0 reduce-scatter.12.cloned.1.call-start
  7.2 34.1 %all_gather.13 = bf16[192,2048]{1,0:T(8,128)(2,1)S(1)} all-gather(bf16[24,2048]{1,0:T(8,128)(2,1)} %param.9), channel_id=1, replica_groups=mesh['row'=8,'col'=4] {'row'}, dimensions={0}, use_global_device_ids=true | all-gather | bytes 884736 | tf_op jit(solution)/shard_map/all_gather | solution.py:55
  41.3 11.7 %fusion.4 = f32[192,3584]{1,0:T(8,128)} fusion(bf16[192,2048]{1,0:T(8,128)(2,1)S(1)} %all_gather.13, bf16[3584,2048]{1,0:T(8,128)(2,1)} %param.8), kind=kOutput, calls=%fused_computation.20 | convolution fusion | flops 2818572288 | bytes 18219008 | tf_op jit(solution)/shard_map/dot_general | solution.py:13
  53.0 0.0 copy-start
  53.0 0.0 reduce-scatter.12.cloned.1.call-update
  53.0 0.0 reduce-scatter.8.cloned.1.call-start
  53.1 0.8 copy-done
  54.0 19.7 %all_to_all.12 = bf16[8,24,2048]{2,1,0:T(8,128)(2,1)S(1)} all-to-all(bf16[8,24,2048]{2,1,0:T(8,128)(2,1)S(1)} %bitcast.24), channel_id=1, replica_groups=mesh['row'=8,'col'=4] {'row'}, dimensions={0} | all-to-all | bytes 1572864 | tf_op jit(solution)/shard_map/all_to_all | solution.py:9
  73.6 9.7 %fusion.2 = f32[192,3584]{1,0:T(8,128)} fusion(bf16[192,2048]{1,0:T(8,128)(2,1)S(1)} %bitcast.20, bf16[2048,3584]{1,0:T(8,128)(2,1)} %param.7), kind=kOutput, calls=%fused_computation.18 | convolution fusion | flops 2818572288 | bytes 18219008 | tf_op jit(solution)/shard_map/dot_general | solution.py:42
  83.4 0.0 reduce-scatter.8.cloned.1.call-update
  83.4 0.0 reduce-scatter.6.cloned.1.call-start
  83.4 9.8 %fusion.1 = f32[192,3584]{1,0:T(8,128)} fusion(bf16[192,2048]{1,0:T(8,128)(2,1)S(1)} %bitcast.21, bf16[2048,3584]{1,0:T(8,128)(2,1)} %param.6), kind=kOutput, calls=%fused_computation.17 | convolution fusion | flops 2818572288 | bytes 18219008 | tf_op jit(solution)/shard_map/dot_general | solution.py:41
  93.2 0.0 reduce-scatter.6.cloned.1.call-update
  93.2 0.0 all-gather.4.cloned.1.call-start
  93.3 0.0 reduce-scatter.12.cloned.1.call-done
  93.3 34.6 %reduce-scatter.8.cloned.1.call-done = f32[48,3584]{1,0:T(8,128)} async-done(((f32[192,3584]{1,0:T(8,128)}), f32[48,3584]{1,0:T(8,128)}) %reduce-scatter.8.cloned.1.call-update) | async-done | bytes 688144 | tf_op jit(solution)/shard_map/reduce_scatter | solution.py:45
  127.9 38.5 %reduce-scatter.6.cloned.1.call-done = f32[48,3584]{1,0:T(8,128)} async-done(((f32[192,3584]{1,0:T(8,128)}), f32[48,3584]{1,0:T(8,128)}) %reduce-scatter.6.cloned.1.call-update) | async-done | bytes 688144 | tf_op jit(solution)/shard_map/reduce_scatter | solution.py:44
  166.5 2.8 multiply_convert_fusion
  169.2 0.0 all-gather.4.cloned.1.call-update
  169.3 0.0 all-gather.6.cloned.1.call-start
  169.3 0.5 all-gather.6.cloned.1.call-update
  169.8 0.0 all-gather.8.cloned.1.call-start
  169.9 0.5 all-gather.8.cloned.1.call-update
  170.4 0.0 reduce-scatter.10.cloned.1.call-start
  170.5 17.5 %all-gather.4.cloned.1.call-done = bf16[192,3584]{1,0:T(8,128)(2,1)} async-done(((bf16[48,3584]{1,0:T(8,128)(2,1)}), bf16[192,3584]{1,0:T(8,128)(2,1)}) %all-gather.4.cloned.1.call-update) | async-done | bytes 1376272 | tf_op jit(solution)/shard_map/all_gather | solution.py:48
  187.9 9.8 %fusion.3 = f32[192,2048]{1,0:T(8,128)} fusion(bf16[192,3584]{1,0:T(8,128)(2,1)} %all-gather.4.cloned.1.call-done, bf16[3584,2048]{1,0:T(8,128)(2,1)} %param.8), kind=kOutput, calls=%fused_computation.19 | convolution fusion | flops 2818572288 | bytes 17629184 | tf_op jit(solution)/shard_map/dot_general | solution.py:50
  197.7 0.0 reduce-scatter.10.cloned.1.call-update
  197.7 0.2 reduce-scatter.14.cloned.1.call-start
  198.0 10.5 %all-gather.6.cloned.1.call-done = bf16[192,3584]{1,0:T(8,128)(2,1)} async-done(((bf16[48,3584]{1,0:T(8,128)(2,1)}), bf16[192,3584]{1,0:T(8,128)(2,1)}) %all-gather.6.cloned.1.call-update) | async-done | bytes 1376272 | tf_op jit(solution)/shard_map/all_gather | solution.py:60
  208.5 11.6 %fusion.5 = f32[192,2048]{1,0:T(8,128)} fusion(bf16[192,3584]{1,0:T(8,128)(2,1)} %all-gather.6.cloned.1.call-done, bf16[2048,3584]{1,0:T(8,128)(2,1)} %param.6), kind=kOutput, calls=%fused_computation.21 | convolution fusion | flops 2818572288 | bytes 17629184 | tf_op jit(solution)/shard_map/dot_general | solution.py:13
  220.1 8.9 %all-gather.8.cloned.1.call-done = bf16[192,3584]{1,0:T(8,128)(2,1)} async-done(((bf16[48,3584]{1,0:T(8,128)(2,1)}), bf16[192,3584]{1,0:T(8,128)(2,1)}) %all-gather.8.cloned.1.call-update) | async-done | bytes 1376272 | tf_op jit(solution)/shard_map/all_gather | solution.py:61
  229.0 0.0 copy-start.3
  229.0 12.1 %convolution_add_fusion = f32[192,2048]{1,0:T(8,128)} fusion(f32[192,2048]{1,0:T(8,128)} %fusion.5, bf16[192,3584]{1,0:T(8,128)(2,1)} %all-gather.8.cloned.1.call-done, bf16[2048,3584]{1,0:T(8,128)(2,1)} %param.7), kind=kOutput, calls=%fused_computation.3 | convolution fusion | flops 2818965504 | bytes 19202048 | tf_op jit(solution)/shard_map/dot_general | solution.py:13
  241.1 0.0 reduce-scatter.14.cloned.1.call-update
  241.2 0.0 copy-done.3
  241.2 0.0 copy-start.2
  241.2 7.6 %convolution_convert_fusion.1 = bf16[2048,3584]{1,0:T(8,128)(2,1)} fusion(bf16[192,2048]{1,0:T(8,128)(2,1)S(1)} %bitcast.22, bf16[192,3584]{1,0:T(8,128)(2,1)S(1)} %copy-done.3), kind=kOutput, calls=%fused_computation.1 | convolution fusion | flops 2825912320 | bytes 16842752 | tf_op jit(solution)/shard_map/dot_general | solution.py:19
  248.8 0.0 copy-done.2
  248.8 0.0 copy-start.1
  248.8 7.6 %convolution_convert_fusion.2 = bf16[2048,3584]{1,0:T(8,128)(2,1)} fusion(bf16[192,2048]{1,0:T(8,128)(2,1)S(1)} %bitcast.23, bf16[192,3584]{1,0:T(8,128)(2,1)S(1)} %copy-done.2), kind=kOutput, calls=%fused_computation.2 | convolution fusion | flops 2825912320 | bytes 16842752 | tf_op jit(solution)/shard_map/dot_general | solution.py:19
  256.4 0.0 copy-done.1
  256.4 7.6 %convolution_convert_fusion = bf16[3584,2048]{1,0:T(8,128)(2,1)} fusion(bf16[192,3584]{1,0:T(8,128)(2,1)S(1)} %copy-done.1, bf16[192,2048]{1,0:T(8,128)(2,1)S(1)} %all_gather.13), kind=kOutput, calls=%fused_computation | convolution fusion | flops 2825912320 | bytes 16842752 | tf_op jit(solution)/shard_map/dot_general | solution.py:19
  264.0 34.2 %reduce-scatter.10.cloned.1.call-done = f32[24,2048]{1,0:T(8,128)} async-done(((f32[192,2048]{1,0:T(8,128)}), f32[24,2048]{1,0:T(8,128)}) %reduce-scatter.10.cloned.1.call-update) | async-done | bytes 196624 | tf_op jit(solution)/shard_map/reduce_scatter | solution.py:49
  298.2 1.6 convert_element_type.25
  299.8 66.4 %reduce-scatter.14.cloned.1.call-done = f32[24,2048]{1,0:T(8,128)} async-done(((f32[192,2048]{1,0:T(8,128)}), f32[24,2048]{1,0:T(8,128)}) %reduce-scatter.14.cloned.1.call-update) | async-done | bytes 196624 | tf_op jit(solution)/shard_map/reduce_scatter | solution.py:63
  366.2 1.6 convert_element_type.28
  (8 shorter events, 0.1 us)
Async XLA Ops:
  7.2 86.1 %reduce-scatter.12.cloned.1.call-start = ((), (), s32[]{:S(2)}) async-start(), calls=%async_computation.10 | async-start | bytes 3440640 | tf_op jit(solution)/shard_map/reduce_scatter | solution.py:57
  53.0 0.9 copy-start
  53.0 74.9 %reduce-scatter.8.cloned.1.call-start = ((), (), s32[]{:S(2)}) async-start(), calls=%async_computation.7 | async-start | bytes 3440640 | tf_op jit(solution)/shard_map/reduce_scatter | solution.py:45
  83.4 83.1 %reduce-scatter.6.cloned.1.call-start = ((), (), s32[]{:S(2)}) async-start(), calls=%async_computation.6 | async-start | bytes 3440640 | tf_op jit(solution)/shard_map/reduce_scatter | solution.py:44
  93.2 94.7 %all-gather.4.cloned.1.call-start = ((), (), s32[]{:S(2)}) async-start(), calls=%async_computation.8 | async-start | bytes 1720320 | tf_op jit(solution)/shard_map/all_gather | solution.py:48
  169.3 39.2 %all-gather.6.cloned.1.call-start = ((), (), s32[]{:S(2)}) async-start(), calls=%async_computation.11 | async-start | bytes 1720320 | tf_op jit(solution)/shard_map/all_gather | solution.py:60
  169.8 59.2 %all-gather.8.cloned.1.call-start = ((), (), s32[]{:S(2)}) async-start(), calls=%async_computation.12 | async-start | bytes 1720320 | tf_op jit(solution)/shard_map/all_gather | solution.py:61
  170.4 127.8 %reduce-scatter.10.cloned.1.call-start = ((), (), s32[]{:S(2)}) async-start(), calls=%async_computation.9 | async-start | bytes 1769472 | tf_op jit(solution)/shard_map/reduce_scatter | solution.py:49
  197.7 168.4 %reduce-scatter.14.cloned.1.call-start = ((), (), s32[]{:S(2)}) async-start(), calls=%async_computation.13 | async-start | bytes 1769472 | tf_op jit(solution)/shard_map/reduce_scatter | solution.py:63
  229.0 12.1 %copy-start.3 = (bf16[192,3584]{1,0:T(8,128)(2,1)S(1)}, bf16[192,3584]{1,0:T(8,128)(2,1)}, u32[]{:S(2)}) copy-start(bf16[192,3584]{1,0:T(8,128)(2,1)} %all-gather.8.cloned.1.call-done) | copy-start | bytes 4128772
  241.2 7.6 %copy-start.2 = (bf16[192,3584]{1,0:T(8,128)(2,1)S(1)}, bf16[192,3584]{1,0:T(8,128)(2,1)}, u32[]{:S(2)}) copy-start(bf16[192,3584]{1,0:T(8,128)(2,1)} %all-gather.6.cloned.1.call-done) | copy-start | bytes 4128772
  248.8 7.6 %copy-start.1 = (bf16[192,3584]{1,0:T(8,128)(2,1)S(1)}, bf16[192,3584]{1,0:T(8,128)(2,1)}, u32[]{:S(2)}) copy-start(bf16[192,3584]{1,0:T(8,128)(2,1)} %all-gather.4.cloned.1.call-done) | copy-start | bytes 4128772
Sparse Core Ops, SparseCore 0:
  53.1 36.2 reduce-scatter.11
  92.6 35.3 reduce-scatter.7
  131.1 35.3 reduce-scatter.5
  169.4 18.5 all-gather.3
  189.9 18.5 all-gather.5
  210.5 18.5 all-gather.7
  232.5 65.7 reduce-scatter.9
  301.6 64.4 reduce-scatter.13
